TPU v7x, 32 devices: a whole 2x2x4 slice. The times are simulated.
32 devices in a mesh: sub: 8 (over z, x), blk: 4 (over y, core).
Axes of the slice: x: 2, y: 2, z: 4, core: 2. Of those that a mesh axis runs over, the one named last changes fastest.
Arguments:
- a_tiles: bfloat16 [768, 12, 128, 128], P(('sub', 'blk'))
- modes: bfloat16 [768, 16, 128], P(('sub', 'blk')), may hold values from -6 to 6
- col_tiles: int32 [768, 12], P(('sub', 'blk')), may hold values from 0 to 221, as said below
- fetch_list: int32 [32, 126], P(('sub', 'blk')), may hold values from 0 to 767, as said below
Outputs:
- prolong: bfloat16 [768, 12, 16, 128], P(('sub', 'blk'))
- coarse_diag: float32 [768, 256], P('sub')
Inputs may be any that keep to these rules, and one draw needn't show every extreme that they name: `col_tiles`: slot 0 of row tile t names t itself (its index within its group); the other slots name other tiles of the same group (values below 96) or 96 + h for entry h of the device's fetch list; every entry of a device's fetch list is named by some slot of that device's rows. `fetch_list`: A device's list is 7 blocks of 18 entries; each block names distinct tiles of one group other than the device's own, different blocks name different groups; tile i of group g has number g * 96 + i.
All inputs are finite; a program needn't handle non-finite values.
Results may differ from a plain program's by a relative error of at most 0.008.
Values may be sent and summed in bfloat16 or wider, within the bound.
No kernel may reach another device: no remote copies, remote signals or barrier semaphores. Data moves between devices by JAX's collectives and lax.ppermute only.
A program may use at most 64 MiB of HBM per device.

v0:
```python
import jax
import jax.numpy as jnp
from jax import lax
from jax.sharding import PartitionSpec as P

NEIGHBOURS = 26
damping = 2.0 / 3.0


def shards(a_tiles, modes, col_tiles, fetch_list):
    blk_count = lax.axis_size("blk")
    sub_count = lax.axis_size("sub")
    tile_dev = a_tiles.shape[0]
    slot_count = a_tiles.shape[1]
    tile_rows = a_tiles.shape[2]
    mode_count = modes.shape[1]
    group_size = tile_dev * blk_count
    ghost_count = fetch_list.shape[1]
    peer_count = min(NEIGHBOURS, sub_count - 1)
    per_peer = ghost_count // peer_count
    group_modes = lax.all_gather(modes, "blk", axis=0, tiled=True)
    wanted = fetch_list[0].reshape(peer_count, per_peer)
    owners = wanted[:, 0] // group_size
    within = wanted % group_size
    selector = (owners[:, None] == jnp.arange(sub_count, dtype=jnp.int32)[None, :]).astype(
        jnp.int32
    )
    requests = jnp.sum(selector[:, :, None] * (within + 1)[:, None, :], axis=0)
    received = lax.all_to_all(requests, "sub", split_axis=0, concat_axis=0, tiled=True)
    present = received > 0
    picked = group_modes[jnp.maximum(received - 1, 0)]
    picked = jnp.where(present[:, :, None, None], picked, jnp.zeros_like(picked))
    returned = lax.all_to_all(picked, "sub", split_axis=0, concat_axis=0, tiled=True)
    returned, received = (returned, received)
    ghosts = returned[owners].reshape(ghost_count, mode_count, tile_rows)
    lookup = jnp.concatenate([group_modes, ghosts], axis=0)
    gathered = lookup[col_tiles]
    product = jnp.einsum("tkrc,tkmc->tkmr", a_tiles, gathered, preferred_element_type=jnp.float32)
    inverse = 1.0 / jnp.diagonal(a_tiles[:, 0], axis1=1, axis2=2).astype(jnp.float32)
    leading = (jnp.arange(slot_count) == 0).astype(jnp.float32)
    prolong = (
        leading[None, :, None, None] * modes.astype(jnp.float32)[:, None]
        - damping * inverse[:, None, None, :] * product
    ).astype(jnp.bfloat16)
    partial_value = (
        jnp.einsum(
            "tkmr,tknr->tkmn", prolong.astype(jnp.float32), product, precision=lax.Precision.HIGHEST
        )
        / tile_rows
    )
    partial_value = partial_value.reshape(tile_dev * slot_count, mode_count * mode_count)
    segment = (
        col_tiles.reshape(-1)[:, None]
        == jnp.arange(group_size + ghost_count, dtype=jnp.int32)[None, :]
    ).astype(jnp.float32)
    slot_sums = jnp.dot(
        segment.T,
        partial_value,
        precision=lax.Precision.HIGHEST,
        preferred_element_type=jnp.float32,
    )
    ghost_sums = slot_sums[group_size:].reshape(peer_count, per_peer, mode_count * mode_count)
    outgoing = jnp.einsum(
        "jp,jmv->pmv", selector.astype(jnp.float32), ghost_sums, precision=lax.Precision.HIGHEST
    )
    incoming = lax.all_to_all(
        outgoing.astype(jnp.bfloat16), "sub", split_axis=0, concat_axis=0, tiled=True
    ).astype(outgoing.dtype)
    target = (
        received[:, :, None] == jnp.arange(1, group_size + 1, dtype=jnp.int32)[None, None, :]
    ).astype(jnp.float32)
    local_sum = slot_sums[:group_size] + jnp.einsum(
        "pmg,pmv->gv", target, incoming, precision=lax.Precision.HIGHEST
    )
    coarse_diag = lax.psum(local_sum.astype(jnp.bfloat16), "blk").astype(jnp.float32)
    return (prolong, coarse_diag)


def solution(mesh):
    in_specs = (
        P(("sub", "blk"), None, None, None),
        P(("sub", "blk"), None, None),
        P(("sub", "blk"), None),
        P(("sub", "blk"), None),
    )
    out_specs = (P(("sub", "blk"), None, None, None), P("sub", None))
    return jax.shard_map(shards, mesh=mesh, in_specs=in_specs, out_specs=out_specs, check_vma=False)
```

profile of v0, /device:TPU:0, one launch (start us, length us, event | category | flops | bytes accessed | tf_op | source)
XLA Modules:
  0.0 80.3 jit_solution(5689057946343639641)
XLA Ops:
  0.6 0.5 broadcast.175
  1.2 1.3 %reduce.11 = s32[126]{0:T(128)S(1)} reduce(s32[1,126]{1,0:T(1,128)} %param.7, s32[]{:T(128)} %broadcast.175), dimensions={0}, to_apply=%param.7.reduce_sub_computation.3 | reduce | bytes 1012 | tf_op args[3]
  2.8 0.7 multiply_reduce_fusion
  3.5 7.3 %all-to-all-start = ((s32[8,1,18]{2,1,0:T(1,128)}), s32[8,1,18]{2,1,0:T(1,128)S(1)}, u32[]{:S(2)}, u32[]{:S(2)}) async-start(s32[8,1,18]{2,1,0:T(1,128)} %bitcast.4), calls=%async_computation | async-start | bytes 8192 | tf_op jit(solution)/shard_map/all_to_all | solution.py:29
  10.8 6.7 %all_gather.3 = bf16[96,16,128]{2,1,0:T(8,128)(2,1)S(1)} all-gather(bf16[24,16,128]{2,1,0:T(8,128)(2,1)} %param.5), channel_id=1, replica_groups=mesh['sub'=8,'blk'=4] {'blk'}, dimensions={0}, use_global_device_ids=true | all-gather | bytes 491520 | tf_op jit(solution)/shard_map/all_gather | solution.py:21
  17.6 0.7 gather_fusion.1
  18.3 1.0 %broadcast_select_fusion = bf16[8,18,16,128]{3,2,1,0:T(8,128)(2,1)} fusion(bf16[8,18,16,128]{3,2,1,0:T(8,128)(2,1)S(1)} %bitcast.31, pred[8,18]{1,0:T(8,128)(4,1)S(1)} %broadcast_compare_fusion), kind=kLoop, calls=%fused_computation.11 | loop fusion | flops 294912 | bytes 1179792 | tf_op jit(solution)/shard_map/jit(_where)/select_n | solution.py:32
  19.4 6.0 %all-to-all-start.1 = ((bf16[8,18,16,128]{3,2,1,0:T(8,128)(2,1)}), bf16[8,18,16,128]{3,2,1,0:T(8,128)(2,1)S(1)}, u32[]{:S(2)}, u32[]{:S(2)}) async-start(bf16[8,18,16,128]{3,2,1,0:T(8,128)(2,1)} %broadcast_select_fusion), calls=%async_computation.1 | async-start | bytes 1179648 | tf_op jit(solution)/shard_map/all_to_all | solution.py:33
  25.4 3.2 %copy.42 = bf16[24,1,128,128]{0,3,2,1:T(8,128)(2,1)} copy(bf16[24,1,128,128]{3,2,1,0:T(8,128)(2,1)S(1)} %slice-done) | data formatting | bytes 1572864
  28.6 1.9 %gather_fusion = bf16[128,24]{1,0:T(8,128)(2,1)S(1)} fusion(bf16[24,128,128]{0,2,1:T(8,128)(2,1)} %bitcast.30, s32[128]{0:T(128)S(1)} %or_bitcast_fusion), kind=kCustom, calls=%fused_computation | custom fusion | bytes 13312 | tf_op jit(solution)/shard_map/jit(diagonal)/gather | solution.py:39
  31.1 10.7 %all-to-all-done.1 = bf16[8,18,16,128]{3,2,1,0:T(8,128)(2,1)S(1)} async-done(((bf16[8,18,16,128]{3,2,1,0:T(8,128)(2,1)}), bf16[8,18,16,128]{3,2,1,0:T(8,128)(2,1)S(1)}, u32[]{:S(2)}, u32[]{:S(2)}) %all-to-all-start.1) | async-done | bytes 589856 | tf_op jit(solution)/shard_map/all_to_all | solution.py:33
  41.8 0.6 gather_fusion.2
  42.5 1.8 %gather_fusion.3 = bf16[288,16,128]{2,1,0:T(8,128)(2,1)S(1)} fusion(bf16[222,16,128]{2,1,0:T(8,128)(2,1)S(1)} %pad_maximum_fusion, s32[1024]{0:T(1024)S(1)} %pad_clamp_fusion), kind=kCustom, calls=%fused_computation.3 | custom fusion | bytes 2360448 | tf_op jit(solution)/shard_map/gather | solution.py:37
  44.4 7.5 %subtract_convert_fusion = (bf16[24,12,16,128]{3,2,1,0:T(8,128)(2,1)S(1)}, f32[24,12,16,128]{3,2,1,0:T(8,128)S(1)}) fusion(f32[24,128]{1,0:T(8,128)S(1)} %multiply_bitcast_fusion, f32[24,16,128]{2,1,0:T(8,128)S(1)} %convert_element_type.44, f32[12]{0:T(128)S(1)} %compare_convert_fusion, bf16[24,12,16,128]{3,2,1,0:T(8,128)(2,1)S(1)} %bitcast.29, ...), kind=kOutput, calls=%fused_computation.4 | convolution fusion | flops 153354240 | bytes 14364720 | tf_op jit(solution)/shard_map/tkrc,tkmc->tkmr/dot_general | solution.py:38
  51.8 2.0 %convolution_multiply_fusion = f32[24,12,16,16]{3,2,1,0:T(8,128)S(1)} fusion(bf16[24,12,16,128]{3,2,1,0:T(8,128)(2,1)S(1)} %get-tuple-element.4, f32[24,12,16,128]{3,2,1,0:T(8,128)S(1)} %get-tuple-element.5), kind=kOutput, calls=%fused_computation.5 | convolution fusion | flops 113319936 | bytes 3833856 | tf_op jit(solution)/shard_map/tkmr,tknr->tkmn/dot_general | solution.py:46
  53.8 1.7 %reshape.91 = f32[288,256]{1,0:T(8,128)} reshape(f32[24,12,16,16]{3,2,1,0:T(8,128)S(1)} %convolution_multiply_fusion) | data formatting | bytes 589824 | tf_op jit(solution)/shard_map/reshape | solution.py:51
  55.5 1.5 %fusion.2 = f32[222,256]{1,0:T(8,128)S(1)} fusion(f32[288,256]{1,0:T(8,128)} %reshape.91, s32[288]{0:T(512)S(1)} %eq.58), kind=kOutput, calls=%fused_computation.13 | convolution fusion | flops 196475328 | bytes 523392 | tf_op jit(solution)/shard_map/dot_general | solution.py:56
  57.1 0.3 convolution_convert_fusion
  57.4 0.7 copy.41
  58.0 3.6 %all-to-all-start.2 = ((bf16[8,18,256]{2,1,0:T(8,128)(2,1)}), bf16[8,18,256]{2,1,0:T(8,128)(2,1)S(1)}, u32[]{:S(2)}, u32[]{:S(2)}) async-start(bf16[8,18,256]{2,1,0:T(8,128)(2,1)} %copy.41), calls=%async_computation.2 | async-start | bytes 196608 | tf_op jit(solution)/shard_map/all_to_all | solution.py:66
  61.7 7.1 %all-to-all-done.2 = bf16[8,18,256]{2,1,0:T(8,128)(2,1)S(1)} async-done(((bf16[8,18,256]{2,1,0:T(8,128)(2,1)}), bf16[8,18,256]{2,1,0:T(8,128)(2,1)S(1)}, u32[]{:S(2)}, u32[]{:S(2)}) %all-to-all-start.2) | async-done | bytes 73760 | tf_op jit(solution)/shard_map/all_to_all | solution.py:66
  68.8 0.3 fusion.1
  69.1 10.5 %psum.7 = bf16[96,256]{1,0:T(8,128)(2,1)S(1)} all-reduce(bf16[96,256]{1,0:T(8,128)(2,1)S(1)} %fusion.1), channel_id=1, replica_groups=mesh['sub'=8,'blk'=4] {'blk'}, use_global_device_ids=true, to_apply=%region_1.2 | all-reduce | flops 24576 | bytes 98304 | tf_op jit(solution)/shard_map/psum | solution.py:75
  79.6 0.6 convert_element_type.51
  (34 shorter events, 1.1 us)
Async XLA Ops:
  0.6 24.7 %copy-start.1 = (bf16[24,16,128]{2,1,0:T(8,128)(2,1)S(1)}, bf16[24,16,128]{2,1,0:T(8,128)(2,1)}, u32[]{:S(2)}) copy-start(bf16[24,16,128]{2,1,0:T(8,128)(2,1)} %param.5) | copy-start | bytes 294916
  3.5 14.0 %all-to-all-start = ((s32[8,1,18]{2,1,0:T(1,128)}), s32[8,1,18]{2,1,0:T(1,128)S(1)}, u32[]{:S(2)}, u32[]{:S(2)}) async-start(s32[8,1,18]{2,1,0:T(1,128)} %bitcast.4), calls=%async_computation | async-start | bytes 8192 | tf_op jit(solution)/shard_map/all_to_all | solution.py:29
  18.3 7.1 %slice-start = ((bf16[24,12,128,128]{3,2,1,0:T(8,128)(2,1)}), bf16[24,1,128,128]{3,2,1,0:T(8,128)(2,1)S(1)}, s32[]{:S(2)}) async-start(bf16[24,12,128,128]{3,2,1,0:T(8,128)(2,1)} %param.4), calls=%async_computation.3 | async-start | bytes 1572864 | tf_op jit(solution)/shard_map/slice | solution.py:39
  19.4 22.4 %all-to-all-start.1 = ((bf16[8,18,16,128]{3,2,1,0:T(8,128)(2,1)}), bf16[8,18,16,128]{3,2,1,0:T(8,128)(2,1)S(1)}, u32[]{:S(2)}, u32[]{:S(2)}) async-start(bf16[8,18,16,128]{3,2,1,0:T(8,128)(2,1)} %broadcast_select_fusion), calls=%async_computation.1 | async-start | bytes 1179648 | tf_op jit(solution)/shard_map/all_to_all | solution.py:33
  25.4 5.3 %copy-start.2 = (s32[24,12]{0,1:T(8,128)S(1)}, s32[24,12]{0,1:T(8,128)}, u32[]{:S(2)}) copy-start(s32[24,12]{0,1:T(8,128)} %param.6) | copy-start | bytes 3460
  51.8 2.0 %copy-start = (bf16[24,12,16,128]{3,2,1,0:T(8,128)(2,1)}, bf16[24,12,16,128]{3,2,1,0:T(8,128)(2,1)S(1)}, u32[]{:S(2)}) copy-start(bf16[24,12,16,128]{3,2,1,0:T(8,128)(2,1)S(1)} %get-tuple-element.4) | copy-start | bytes 3538948
  58.0 10.8 %all-to-all-start.2 = ((bf16[8,18,256]{2,1,0:T(8,128)(2,1)}), bf16[8,18,256]{2,1,0:T(8,128)(2,1)S(1)}, u32[]{:S(2)}, u32[]{:S(2)}) async-start(bf16[8,18,256]{2,1,0:T(8,128)(2,1)} %copy.41), calls=%async_computation.2 | async-start | bytes 196608 | tf_op jit(solution)/shard_map/all_to_all | solution.py:66
where the time goes:
time: 80.7 us; the launch traced here: 80.3 us
  waiting for transfers between devices  17.8 us (22%)
  blocking collectives  17.2 us (21%)
  starting transfers between devices  16.9 us (21%)
  local copies, waits for them, and re-layouts  12 us (15%)
  matrix products  11.6 us (14%)
  other arithmetic  4.03 us (5%)
  between operations  0.83 us (1%)
    all_to_all x1, waiting for transfers between devices, shards(): lax.all_to_all(picked, 'sub', split_axis=0, concat_axis=0, tiled=True)  10.7 us
    psum x1, blocking collectives, shards(): lax.psum(local_sum.astype(jnp.bfloat16), 'blk').astype(jnp.float32)  10.5 us
    dot_general x1, matrix products, shards(): jnp.einsum('tkrc,tkmc->tkmr', a_tiles, gathered, preferred_element_type=j...  7.47 us
    all_to_all x1, starting transfers between devices, shards(): lax.all_to_all(requests, 'sub', split_axis=0, concat_axis=0, tiled=True)  7.28 us
    all_to_all x1, waiting for transfers between devices, shards(): lax.all_to_all(outgoing.astype(jnp.bfloat16), 'sub', split_axis=0, concat...  7.12 us
    all_gather x1, blocking collectives, shards(): group_modes = lax.all_gather(modes, 'blk', axis=0, tiled=True)  6.68 us
    all_to_all x1, starting transfers between devices, shards(): lax.all_to_all(picked, 'sub', split_axis=0, concat_axis=0, tiled=True)  5.99 us
    unnamed x9, local copies, waits for them, and re-layouts  3.84 us
  transfers between devices with their start and end apart: 3, of which 2 were waited for; matrix products, arithmetic and copies ran while one was open for 7% of the time, Pallas kernels for 0%

commit v1 on v0

--- a/solution.py
+++ b/solution.py
@@ -18,7 +18,21 @@
     ghost_count = fetch_list.shape[1]
     peer_count = min(NEIGHBOURS, sub_count - 1)
     per_peer = ghost_count // peer_count
-    group_modes = lax.all_gather(modes, "blk", axis=0, tiled=True)
+    ways, here, step = (lax.axis_size("blk"), lax.axis_index("blk"), modes.shape[0])
+    shape = [n * ways if d == 0 else n for d, n in enumerate(modes.shape)]
+    full = lax.dynamic_update_slice_in_dim(
+        jnp.zeros(shape, modes.dtype), modes, here * step, axis=0
+    )
+    going_up = going_down = modes
+    for far in range(1, ways // 2 + 1):
+        going_up = lax.ppermute(going_up, "blk", [(d, (d + 1) % ways) for d in range(ways)])
+        full = lax.dynamic_update_slice_in_dim(full, going_up, (here - far) % ways * step, axis=0)
+        if 2 * far < ways:
+            going_down = lax.ppermute(going_down, "blk", [(d, (d - 1) % ways) for d in range(ways)])
+            full = lax.dynamic_update_slice_in_dim(
+                full, going_down, (here + far) % ways * step, axis=0
+            )
+    group_modes = full
     wanted = fetch_list[0].reshape(peer_count, per_peer)
     owners = wanted[:, 0] // group_size
     within = wanted % group_size

time: 80.7 us -> 83.2 us (1.031)
  waiting for transfers between devices: 17.8 us -> 26.2 us
  blocking collectives: 17.2 us -> 10.8 us
  other arithmetic: 4.03 us -> 5.02 us
    all_gather x1 -> x0, blocking collectives: 6.68 us -> none  [shards(): group_modes = lax.all_gather(modes, 'blk', axis=0, tiled=True)]
    all_to_all x1, waiting for transfers between devices: 0.01 us -> 5.32 us  [shards(): lax.all_to_all(requests, 'sub', split_axis=0, concat_axis=0, tiled=True)]
    ppermute x0 -> x3, waiting for transfers between devices: none -> 3.97 us  [the longest x2 3.97 us: shards(): lax.ppermute(going_up, 'blk', [(d, (d + 1) % ways) for d in range(ways)])]
    ppermute x0 -> x3, starting transfers between devices: none -> 2.61 us  [the longest x1 2.01 us: shards(): lax.ppermute(going_down, 'blk', [(d, (d - 1) % ways) for d in range(ways)])]
    all_to_all x1, starting transfers between devices: 5.99 us -> 3.54 us  [shards(): lax.all_to_all(picked, 'sub', split_axis=0, concat_axis=0, tiled=True)]
    convert_element_type x1, other arithmetic: 0.02 us -> 1 us  [shards(): modes.astype(jnp.float32)[:, None]]
    all_to_all x1, waiting for transfers between devices: 10.7 us -> 9.77 us  [shards(): lax.all_to_all(picked, 'sub', split_axis=0, concat_axis=0, tiled=True)]
    unnamed x9 -> x7, local copies, waits for them, and re-layouts: 3.84 us -> 3.84 us
  transfers between devices with their start and end apart: 3 -> 6, of which waited for: 2 -> 4; matrix products, arithmetic and copies ran while one was open for 7% -> 12% of each run, Pallas kernels for 0% -> 0%
where the time goes in v1:
time: 83.2 us; the launch traced here: 82.8 us
  waiting for transfers between devices  26.2 us (31%)
  starting transfers between devices  16.3 us (20%)
  local copies, waits for them, and re-layouts  12.1 us (15%)
  matrix products  11.6 us (14%)
  blocking collectives  10.8 us (13%)
  other arithmetic  5.02 us (6%)
  between operations  0.91 us (1%)
    psum x1, blocking collectives, shards(): lax.psum(local_sum.astype(jnp.bfloat16), 'blk').astype(jnp.float32)  10.8 us
    all_to_all x1, waiting for transfers between devices, shards(): lax.all_to_all(picked, 'sub', split_axis=0, concat_axis=0, tiled=True)  9.77 us
    dot_general x1, matrix products, shards(): jnp.einsum('tkrc,tkmc->tkmr', a_tiles, gathered, preferred_element_type=j...  7.47 us
    all_to_all x1, waiting for transfers between devices, shards(): lax.all_to_all(outgoing.astype(jnp.bfloat16), 'sub', split_axis=0, concat...  7.12 us
    all_to_all x1, starting transfers between devices, shards(): lax.all_to_all(requests, 'sub', split_axis=0, concat_axis=0, tiled=True)  6.53 us
    all_to_all x1, waiting for transfers between devices, shards(): lax.all_to_all(requests, 'sub', split_axis=0, concat_axis=0, tiled=True)  5.32 us
    ppermute x2, waiting for transfers between devices, shards(): lax.ppermute(going_up, 'blk', [(d, (d + 1) % ways) for d in range(ways)])  3.97 us
    unnamed x7, local copies, waits for them, and re-layouts  3.84 us
  transfers between devices with their start and end apart: 6, of which 4 were waited for; matrix products, arithmetic and copies ran while one was open for 12% of the time, Pallas kernels for 0%

profile of v1, /device:TPU:0, one launch (start us, length us, event | category | flops | bytes accessed | tf_op | source)
XLA Modules:
  0.0 82.8 jit_solution(17203313170105914707)
XLA Ops:
  1.2 2.0 %collective-permute-start.1 = (bf16[24,16,128]{2,1,0:T(8,128)(2,1)}, bf16[24,16,128]{2,1,0:T(8,128)(2,1)S(1)}, u32[]{:S(2)}, u32[]{:S(2)}) collective-permute-start(bf16[24,16,128]{2,1,0:T(8,128)(2,1)} %param.5), channel_id=1, source_target_pairs={{0,3},{1,0},{2,1},{3,2},{4,7},{5,4},{6,5},{7,6},{8,11},{9,8},{10,9... | collective-permute-start | bytes 294920 | tf_op jit(solution)/shard_map/ppermute | solution.py:31
  3.7 1.3 %reduce.11 = s32[126]{0:T(128)S(1)} reduce(s32[1,126]{1,0:T(1,128)} %param.7, s32[]{:T(128)} %broadcast.178), dimensions={0}, to_apply=%param.7.reduce_sub_computation.3 | reduce | bytes 1012 | tf_op args[3]
  5.4 0.7 multiply_reduce_fusion
  6.0 6.5 %all-to-all-start = ((s32[8,1,18]{2,1,0:T(1,128)}), s32[8,1,18]{2,1,0:T(1,128)S(1)}, u32[]{:S(2)}, u32[]{:S(2)}) async-start(s32[8,1,18]{2,1,0:T(1,128)} %bitcast.4), calls=%async_computation | async-start | bytes 8192 | tf_op jit(solution)/shard_map/all_to_all | solution.py:43
  12.6 1.0 %fusion.16 = (f32[24,16,128]{2,1,0:T(8,128)S(1)}, bf16[96,16,128]{2,1,0:T(8,128)(2,1)S(1)}) fusion(bf16[24,16,128]{2,1,0:T(8,128)(2,1)} %param.5, bf16[96,16,128]{2,1,0:T(8,128)(2,1)S(1)} %broadcast_in_dim.16, s32[]{:T(128)S(6)} %select_n.62), kind=kLoop, calls=%fused_computation.47 | loop fusion | flops 49152 | bytes 393220 | tf_op jit(solution)/shard_map/convert_element_type | solution.py:56
  13.7 5.3 %all-to-all-done = s32[8,1,18]{2,1,0:T(1,128)S(1)} async-done(((s32[8,1,18]{2,1,0:T(1,128)}), s32[8,1,18]{2,1,0:T(1,128)S(1)}, u32[]{:S(2)}, u32[]{:S(2)}) %all-to-all-start) | async-done | bytes 608 | tf_op jit(solution)/shard_map/all_to_all | solution.py:43
  19.2 4.0 %collective-permute-done.2 = bf16[24,16,128]{2,1,0:T(8,128)(2,1)S(1)} collective-permute-done((bf16[24,16,128]{2,1,0:T(8,128)(2,1)S(1)}, bf16[24,16,128]{2,1,0:T(8,128)(2,1)S(1)}, u32[]{:S(2)}, u32[]{:S(2)}) %collective-permute-start.2) | collective-permute-done | bytes 98336 | tf_op jit(solution)/shard_map/ppermute | solution.py:28
  23.2 0.7 gather_fusion.1
  24.0 1.0 %broadcast_select_fusion = bf16[8,18,16,128]{3,2,1,0:T(8,128)(2,1)} fusion(bf16[8,18,16,128]{3,2,1,0:T(8,128)(2,1)S(1)} %bitcast.31, pred[8,18]{1,0:T(8,128)(4,1)S(1)} %broadcast_compare_fusion), kind=kLoop, calls=%fused_computation.11 | loop fusion | flops 294912 | bytes 1179792 | tf_op jit(solution)/shard_map/jit(_where)/select_n | solution.py:46
  25.0 3.5 %all-to-all-start.1 = ((bf16[8,18,16,128]{3,2,1,0:T(8,128)(2,1)}), bf16[8,18,16,128]{3,2,1,0:T(8,128)(2,1)S(1)}, u32[]{:S(2)}, u32[]{:S(2)}) async-start(bf16[8,18,16,128]{3,2,1,0:T(8,128)(2,1)} %broadcast_select_fusion), calls=%async_computation.1 | async-start | bytes 1179648 | tf_op jit(solution)/shard_map/all_to_all | solution.py:47
  28.6 3.2 %copy.42 = bf16[24,1,128,128]{0,3,2,1:T(8,128)(2,1)} copy(bf16[24,1,128,128]{3,2,1,0:T(8,128)(2,1)S(1)} %slice-done) | data formatting | bytes 1572864
  31.8 1.9 %gather_fusion = bf16[128,24]{1,0:T(8,128)(2,1)S(1)} fusion(bf16[24,128,128]{0,2,1:T(8,128)(2,1)} %bitcast.30, s32[128]{0:T(128)S(1)} %or_bitcast_fusion), kind=kCustom, calls=%fused_computation | custom fusion | bytes 13312 | tf_op jit(solution)/shard_map/jit(diagonal)/gather | solution.py:53
  34.3 9.8 %all-to-all-done.1 = bf16[8,18,16,128]{3,2,1,0:T(8,128)(2,1)S(1)} async-done(((bf16[8,18,16,128]{3,2,1,0:T(8,128)(2,1)}), bf16[8,18,16,128]{3,2,1,0:T(8,128)(2,1)S(1)}, u32[]{:S(2)}, u32[]{:S(2)}) %all-to-all-start.1) | async-done | bytes 589856 | tf_op jit(solution)/shard_map/all_to_all | solution.py:47
  44.1 0.6 gather_fusion.2
  44.8 1.8 %gather_fusion.3 = bf16[288,16,128]{2,1,0:T(8,128)(2,1)S(1)} fusion(bf16[222,16,128]{2,1,0:T(8,128)(2,1)S(1)} %pad_maximum_fusion, s32[1024]{0:T(1024)S(1)} %pad_clamp_fusion), kind=kCustom, calls=%fused_computation.3 | custom fusion | bytes 2360448 | tf_op jit(solution)/shard_map/gather | solution.py:51
  46.6 7.5 %subtract_convert_fusion = (bf16[24,12,16,128]{3,2,1,0:T(8,128)(2,1)S(1)}, f32[24,12,16,128]{3,2,1,0:T(8,128)S(1)}) fusion(f32[24,128]{1,0:T(8,128)S(1)} %multiply_bitcast_fusion, f32[24,16,128]{2,1,0:T(8,128)S(1)} %get-tuple-element.4, f32[12]{0:T(128)S(1)} %compare_convert_fusion, bf16[24,12,16,128]{3,2,1,0:T(8,128)(2,1)S(1)} %bitcast.29, ...), kind=kOutput, calls=%fused_computation.4 | convolution fusion | flops 153354240 | bytes 14364720 | tf_op jit(solution)/shard_map/tkrc,tkmc->tkmr/dot_general | solution.py:52
  54.1 2.0 %convolution_multiply_fusion = f32[24,12,16,16]{3,2,1,0:T(8,128)S(1)} fusion(bf16[24,12,16,128]{3,2,1,0:T(8,128)(2,1)S(1)} %get-tuple-element.6, f32[24,12,16,128]{3,2,1,0:T(8,128)S(1)} %get-tuple-element.7), kind=kOutput, calls=%fused_computation.5 | convolution fusion | flops 113319936 | bytes 3833856 | tf_op jit(solution)/shard_map/tkmr,tknr->tkmn/dot_general | solution.py:60
  56.1 1.7 %reshape.91 = f32[288,256]{1,0:T(8,128)} reshape(f32[24,12,16,16]{3,2,1,0:T(8,128)S(1)} %convolution_multiply_fusion) | data formatting | bytes 589824 | tf_op jit(solution)/shard_map/reshape | solution.py:65
  57.8 1.5 %fusion.2 = f32[222,256]{1,0:T(8,128)S(1)} fusion(f32[288,256]{1,0:T(8,128)} %reshape.91, s32[288]{0:T(512)S(1)} %eq.62), kind=kOutput, calls=%fused_computation.13 | convolution fusion | flops 196475328 | bytes 523392 | tf_op jit(solution)/shard_map/dot_general | solution.py:70
  59.7 0.7 copy.41
  60.3 3.6 %all-to-all-start.2 = ((bf16[8,18,256]{2,1,0:T(8,128)(2,1)}), bf16[8,18,256]{2,1,0:T(8,128)(2,1)S(1)}, u32[]{:S(2)}, u32[]{:S(2)}) async-start(bf16[8,18,256]{2,1,0:T(8,128)(2,1)} %copy.41), calls=%async_computation.2 | async-start | bytes 196608 | tf_op jit(solution)/shard_map/all_to_all | solution.py:80
  63.9 7.1 %all-to-all-done.2 = bf16[8,18,256]{2,1,0:T(8,128)(2,1)S(1)} async-done(((bf16[8,18,256]{2,1,0:T(8,128)(2,1)}), bf16[8,18,256]{2,1,0:T(8,128)(2,1)S(1)}, u32[]{:S(2)}, u32[]{:S(2)}) %all-to-all-start.2) | async-done | bytes 73760 | tf_op jit(solution)/shard_map/all_to_all | solution.py:80
  71.3 10.8 %psum.7 = bf16[96,256]{1,0:T(8,128)(2,1)S(1)} all-reduce(bf16[96,256]{1,0:T(8,128)(2,1)S(1)} %fusion.1), channel_id=1, replica_groups=mesh['sub'=8,'blk'=4] {'blk'}, use_global_device_ids=true, to_apply=%region_1.2 | all-reduce | flops 24576 | bytes 98304 | tf_op jit(solution)/shard_map/psum | solution.py:89
  82.1 0.6 convert_element_type.51
  (41 shorter events, 2.9 us)
Async XLA Ops:
  0.6 18.5 %collective-permute-start = (bf16[24,16,128]{2,1,0:T(8,128)(2,1)}, bf16[24,16,128]{2,1,0:T(8,128)(2,1)S(1)}, u32[]{:S(2)}, u32[]{:S(2)}) collective-permute-start(bf16[24,16,128]{2,1,0:T(8,128)(2,1)} %param.5), channel_id=1, source_target_pairs={{0,1},{1,2},{2,3},{3,0},{4,5},{5,6},{6,7},{7,4},{8,9},{9,10},{10,1... | collective-permute-start | bytes 294920 | tf_op jit(solution)/shard_map/ppermute | solution.py:28
  1.2 18.0 %collective-permute-start.1 = (bf16[24,16,128]{2,1,0:T(8,128)(2,1)}, bf16[24,16,128]{2,1,0:T(8,128)(2,1)S(1)}, u32[]{:S(2)}, u32[]{:S(2)}) collective-permute-start(bf16[24,16,128]{2,1,0:T(8,128)(2,1)} %param.5), channel_id=1, source_target_pairs={{0,3},{1,0},{2,1},{3,2},{4,7},{5,4},{6,5},{7,6},{8,11},{9,8},{10,9... | collective-permute-start | bytes 294920 | tf_op jit(solution)/shard_map/ppermute | solution.py:31
  6.0 12.9 %all-to-all-start = ((s32[8,1,18]{2,1,0:T(1,128)}), s32[8,1,18]{2,1,0:T(1,128)S(1)}, u32[]{:S(2)}, u32[]{:S(2)}) async-start(s32[8,1,18]{2,1,0:T(1,128)} %bitcast.4), calls=%async_computation | async-start | bytes 8192 | tf_op jit(solution)/shard_map/all_to_all | solution.py:43
  19.1 4.1 %collective-permute-start.2 = (bf16[24,16,128]{2,1,0:T(8,128)(2,1)S(1)}, bf16[24,16,128]{2,1,0:T(8,128)(2,1)S(1)}, u32[]{:S(2)}, u32[]{:S(2)}) collective-permute-start(bf16[24,16,128]{2,1,0:T(8,128)(2,1)S(1)} %collective-permute-done), channel_id=1, source_target_pairs={{0,1},{1,2},{2,3},{3,0},{4,5},{5,6},{6,7},{7,4},{8,9},{9,10},{10,1... | collective-permute-start | bytes 294920 | tf_op jit(solution)/shard_map/ppermute | solution.py:28
  23.2 5.3 %slice-start = ((bf16[24,12,128,128]{3,2,1,0:T(8,128)(2,1)}), bf16[24,1,128,128]{3,2,1,0:T(8,128)(2,1)S(1)}, s32[]{:S(2)}) async-start(bf16[24,12,128,128]{3,2,1,0:T(8,128)(2,1)} %param.4), calls=%async_computation.3 | async-start | bytes 1572864 | tf_op jit(solution)/shard_map/slice | solution.py:53
  25.0 19.0 %all-to-all-start.1 = ((bf16[8,18,16,128]{3,2,1,0:T(8,128)(2,1)}), bf16[8,18,16,128]{3,2,1,0:T(8,128)(2,1)S(1)}, u32[]{:S(2)}, u32[]{:S(2)}) async-start(bf16[8,18,16,128]{3,2,1,0:T(8,128)(2,1)} %broadcast_select_fusion), calls=%async_computation.1 | async-start | bytes 1179648 | tf_op jit(solution)/shard_map/all_to_all | solution.py:47
  28.6 5.3 %copy-start.1 = (s32[24,12]{0,1:T(8,128)S(1)}, s32[24,12]{0,1:T(8,128)}, u32[]{:S(2)}) copy-start(s32[24,12]{0,1:T(8,128)} %param.6) | copy-start | bytes 3460
  54.1 2.0 %copy-start = (bf16[24,12,16,128]{3,2,1,0:T(8,128)(2,1)}, bf16[24,12,16,128]{3,2,1,0:T(8,128)(2,1)S(1)}, u32[]{:S(2)}) copy-start(bf16[24,12,16,128]{3,2,1,0:T(8,128)(2,1)S(1)} %get-tuple-element.6) | copy-start | bytes 3538948
  60.3 10.7 %all-to-all-start.2 = ((bf16[8,18,256]{2,1,0:T(8,128)(2,1)}), bf16[8,18,256]{2,1,0:T(8,128)(2,1)S(1)}, u32[]{:S(2)}, u32[]{:S(2)}) async-start(bf16[8,18,256]{2,1,0:T(8,128)(2,1)} %copy.41), calls=%async_computation.2 | async-start | bytes 196608 | tf_op jit(solution)/shard_map/all_to_all | solution.py:80
